TPU v7x, 32 devices: a whole 2x2x4 slice. The times are simulated.
32 devices in a mesh: grp: 8 (over z, core), dev: 4 (over y, x).
Axes of the slice: x: 2, y: 2, z: 4, core: 2. Of those that a mesh axis runs over, the one named last changes fastest.
Arguments:
- query_hidden: bfloat16 [32, 32, 3584], P(('grp', 'dev')), may hold values from -6 to 6
- projection: bfloat16 [3584, 128], replicated, may hold values from -0.09375 to 0.09375
- page_embed: bfloat16 [32, 1024, 128], P('grp', 'dev'), may hold values from -6 to 6
- page_counts: int32 [32], replicated, may hold values from 128 to 1024, as said below
- positive: int32 [32], replicated, may hold values from 0 to 31
- hard_negs: int32 [32, 2], replicated, may hold values from 0 to 31
- loss_weight: float32 [32], replicated, may hold values from 0.5 to 2
Outputs:
- losses: float32 [32], P(('grp', 'dev'))
- hidden_grad: bfloat16 [32, 32, 3584], P(('grp', 'dev'))
- proj_grad: float32 [3584, 128], P(('grp', 'dev'))
- pages_grad: bfloat16 [32, 1024, 128], P('grp', 'dev')
Inputs may be any that keep to these rules, and one draw needn't show every extreme that they name: The first page_counts[p] tokens of page p are valid; some page has all 1024 tokens valid. `hard_negs`: a hard negative may repeat or equal the positive page.
All inputs are finite; a program needn't handle non-finite values.
Results may differ from a plain program's by a relative error of at most 0.018.
Values may be sent and summed in bfloat16 or wider, within the bound.
A program may use at most 64 MiB of HBM per device.

v0:
```python
import functools
import math

import jax
import jax.numpy as jnp
from jax import lax
from jax.experimental import pallas as pl
from jax.experimental.pallas import tpu as pltpu
from jax.sharding import PartitionSpec as P

SOFTMAX_HEAT = 0.02
EPSILON = 1e-06
MESH = pl.DeviceIdType.MESH
NT = (((1,), (1,)), ((), ()))
F32 = jnp.float32
BF16 = jnp.bfloat16


def split3(x):
    a = x.astype(BF16)
    r = x - a.astype(F32)
    b = r.astype(BF16)
    c = (r - b.astype(F32)).astype(BF16)
    return a, b, c


def dot3(x, ind):
    a, b, c = split3(x)
    return (
        jnp.dot(c, ind, preferred_element_type=F32)
        + jnp.dot(b, ind, preferred_element_type=F32)
        + jnp.dot(a, ind, preferred_element_type=F32)
    )


def kernel(
    groups, members, qlen, nhn, nb,
    hid_in, proj_in, page_in, counts_in, crow_in, pos_in, neg_in, lw_in,
    loss_ref, hgrad_ref, pgrad_ref, pagegrad_ref,
    qsend, qall, pn, pscale, ebuf, tot, tx, tall, lgbuf, sc, sc_all, sgbuf, ind_down, ind_up, hsplit, hall, hallt, projt,
    wbuf, qg, rs, rg, rg_all,
    send_sems, recv_sems,
    hid_ref, proj_ref, page_ref, counts_ref, crow_ref, pos_ref, neg_ref, lw_ref, load_sems,
):
    loads = [
        pltpu.make_async_copy(src, dst, load_sems.at[i])
        for i, (src, dst) in enumerate(
            (
                (hid_in, hid_ref), (proj_in, proj_ref), (page_in, page_ref), (counts_in, counts_ref),
                (crow_in, crow_ref), (pos_in, pos_ref), (neg_in, neg_ref), (lw_in, lw_ref),
            )
        )
    ]
    for load in loads:
        load.start()

    n = groups * members
    rows, hidden = hid_ref.shape
    pages_here, slice_len, dim = page_ref.shape
    n_chunks = n // nb
    cq = nb * rows
    q_here = rows // qlen
    q_total = n * q_here
    hb = hidden // n
    gi = lax.axis_index("grp")
    mi = lax.axis_index("dev")
    me = gi * members + mi
    pair = hall.shape[0]
    core = lax.rem(gi, pair)
    chip = lax.div(gi, pair) * members + mi
    chips = n // pair

    def target(k):
        dst = lax.rem(me + k, n)
        return dst, (lax.div(dst, members), lax.rem(dst, members))

    barrier = pltpu.get_barrier_semaphore()

    def greet(k, carry):
        _, where = target(k)
        pl.semaphore_signal(barrier, inc=1, device_id=where, device_id_type=MESH)
        return carry

    lax.fori_loop(1, n, greet, 0)

    def done(ref, sem):
        pltpu.make_async_copy(ref, ref, sem).wait()

    for load in loads:
        load.wait()

    query_raw = jnp.dot(hid_ref[...], proj_ref[...], preferred_element_type=F32)
    query_scale = lax.rsqrt(jnp.sum(query_raw * query_raw, axis=-1, keepdims=True) + EPSILON)
    query_unit = query_raw * query_scale
    qsend[...] = query_unit.astype(BF16)

    for p in range(pages_here):
        praw = page_ref[p].astype(F32)
        ps = lax.rsqrt(jnp.sum(praw * praw, axis=-1, keepdims=True) + EPSILON)
        pscale[p] = ps
        pn[p] = (praw * ps).astype(BF16)

    for j in range(n):
        hsplit[j, :, :hb] = hid_ref[:, j * hb : (j + 1) * hb]
    if hsplit.shape[2] > hb:
        hsplit[:, :, hb:] = jnp.zeros((n, rows, hsplit.shape[2] - hb), BF16)

    projt[...] = jnp.transpose(proj_ref[...])

    def indicators(c, carry):
        r = lax.broadcasted_iota(jnp.int32, (cq, q_total), 0) + c * cq
        q = lax.broadcasted_iota(jnp.int32, (cq, q_total), 1)
        ind_down[c] = jnp.where((r >= q * qlen) & (r < (q + 1) * qlen), 1.0, 0.0).astype(BF16)
        r = lax.broadcasted_iota(jnp.int32, (q_total, cq), 1) + c * cq
        q = lax.broadcasted_iota(jnp.int32, (q_total, cq), 0)
        ind_up[c] = jnp.where((r >= q * qlen) & (r < (q + 1) * qlen), 1.0, 0.0).astype(BF16)
        return carry

    lax.fori_loop(0, n_chunks, indicators, 0)

    pl.semaphore_wait(barrier, n - 1)

    own = pltpu.make_async_copy(qsend, qall.at[me], recv_sems.at[0])
    own.start()

    def send_q(k, carry):
        _, where = target(k)
        pltpu.make_async_remote_copy(
            qsend, qall.at[me], send_sems.at[0], recv_sems.at[0], device_id=where, device_id_type=MESH
        ).start()
        return carry

    lax.fori_loop(1, n, send_q, 0)

    pnt = jnp.transpose(pn[...].reshape(pages_here * slice_len, dim).astype(F32)).astype(BF16)

    done(qall, recv_sems.at[0])

    own_h = pltpu.make_async_copy(hsplit.at[me], hall.at[core, chip], recv_sems.at[3])
    own_h.start()

    def send_h(k, carry):
        dst, where = target(k)
        pltpu.make_async_remote_copy(
            hsplit.at[dst], hall.at[core, chip], send_sems.at[3], recv_sems.at[3], device_id=where, device_id_type=MESH
        ).start()
        return carry

    lax.fori_loop(1, n, send_h, 0)


    token = lax.broadcasted_iota(jnp.int32, (slice_len, 1), 0) + mi * slice_len
    biases = []
    for p in range(pages_here):
        count = counts_ref[gi * pages_here + p]
        biases.append(jnp.where(token < count, 0.0, -1e30).astype(F32))

    def forward(c, carry):
        qc = qall[pl.ds(c * nb, nb)].reshape(cq, dim)
        parts = []
        for p in range(pages_here):
            s = lax.dot_general(pn[p], qc, NT, preferred_element_type=F32)
            e = jnp.exp(s * (1.0 / SOFTMAX_HEAT) + biases[p])
            ebuf[c, p] = e
            parts.append(jnp.sum(e, axis=0, keepdims=True))
        tot[:, pl.ds(pl.multiple_of(c * cq, cq), cq)] = jnp.concatenate(parts, axis=0)
        return carry

    lax.fori_loop(0, n_chunks, forward, 0)

    tx[...] = tot[...].astype(BF16)

    own = pltpu.make_async_copy(tx, tall.at[mi], recv_sems.at[1])
    own.start()
    for k in range(1, members):
        pltpu.make_async_remote_copy(
            tx, tall.at[mi], send_sems.at[1], recv_sems.at[1],
            device_id=(gi, lax.rem(mi + k, members)), device_id_type=MESH,
        ).start()

    page_total = groups * pages_here
    pos_row = pos_ref[...].astype(F32)
    neg_rows = [neg_ref[j : j + 1, :].astype(F32) for j in range(nhn)]
    lw_row = lw_ref[...]
    eye = lax.broadcasted_iota(jnp.int32, (page_total, page_total), 0) == lax.broadcasted_iota(
        jnp.int32, (page_total, page_total), 1
    )
    count_col = jnp.sum(jnp.where(eye, crow_ref[...].astype(F32), 0.0), axis=1, keepdims=True)
    log_count = (SOFTMAX_HEAT * qlen) * jnp.log(count_col)
    page_id = lax.broadcasted_iota(jnp.int32, (page_total, q_total), 0).astype(F32)
    pos_hot = jnp.where(page_id == pos_row, 1.0, 0.0)
    neg_hots = [jnp.where(page_id == row, 1.0, 0.0) for row in neg_rows]

    done(tall, recv_sems.at[1])

    total = tall[0].astype(F32)
    for k in range(1, members):
        total = total + tall[k].astype(F32)
    tot[...] = total
    lgbuf[...] = jnp.log(total)

    def compress(c, acc):
        at = pl.ds(c * cq if isinstance(c, int) else pl.multiple_of(c * cq, cq), cq)
        return acc + dot3(lgbuf[:, at], ind_down[c])

    acc = jnp.zeros((pages_here, q_total), F32)
    if n_chunks <= 8:
        for c in range(n_chunks):
            acc = compress(c, acc)
    else:
        acc = lax.fori_loop(0, n_chunks, compress, acc)
    sc[...] = SOFTMAX_HEAT * acc

    own_s = pltpu.make_async_copy(sc, sc_all.at[gi], recv_sems.at[2])
    own_s.start()
    for k in range(1, groups):
        pltpu.make_async_remote_copy(
            sc, sc_all.at[gi], send_sems.at[2], recv_sems.at[2],
            device_id=(lax.rem(gi + k, groups), mi), device_id_type=MESH,
        ).start()
    done(sc_all, recv_sems.at[2])
    scores = jnp.concatenate([sc_all[g] for g in range(groups)], axis=0) - log_count

    log_total = jnp.log(jnp.sum(jnp.exp(scores), axis=0, keepdims=True))
    pos_score = jnp.sum(scores * pos_hot, axis=0, keepdims=True)
    soft = jnp.zeros((1, q_total), F32)
    push = jnp.zeros((page_total, q_total), F32)
    for j in range(nhn):
        margin = jnp.sum(scores * neg_hots[j], axis=0, keepdims=True) - pos_score
        small = jnp.exp(-jnp.abs(margin))
        soft = soft + jnp.maximum(margin, 0.0) + jnp.log1p(small)
        sig = jnp.where(margin >= 0, 1.0, small) / (1.0 + small)
        push = push + sig * (neg_hots[j] - pos_hot)
    losses = log_total - pos_score + soft / nhn
    grads = lw_row * (jnp.exp(scores - log_total) - pos_hot + push / nhn)
    for g in range(groups):
        sgbuf[g] = grads[g * pages_here : (g + 1) * pages_here, :]
    score_grad = sgbuf[gi]
    lane = lax.broadcasted_iota(jnp.int32, (1, q_total), 1)
    for i in range(q_here):
        loss_ref[i] = jnp.sum(jnp.where(lane == me * q_here + i, losses, 0.0))

    grad3 = split3(score_grad)
    first_chunk = lax.div(me, nb)

    def backward(i, carry):
        c = lax.rem(first_chunk + i, n_chunks)
        ind = ind_up[c]
        wide = (
            jnp.dot(grad3[2], ind, preferred_element_type=F32)
            + jnp.dot(grad3[1], ind, preferred_element_type=F32)
            + jnp.dot(grad3[0], ind, preferred_element_type=F32)
        )
        factor = wide / tot[:, pl.ds(pl.multiple_of(c * cq, cq), cq)]
        for p in range(pages_here):
            wbuf[c, p] = (ebuf[c, p] * factor[p : p + 1, :]).astype(BF16)
        w = wbuf[c].reshape(pages_here * slice_len, cq)
        gt = jnp.dot(pnt, w, preferred_element_type=F32)
        qg[pl.ds(c * nb, nb)] = jnp.transpose(gt).astype(BF16).reshape(nb, rows, dim)

        def send(k, carry2):
            dst = c * nb + k
            where = (lax.div(dst, members), lax.rem(dst, members))

            @pl.when(dst != me)
            def _():
                pltpu.make_async_remote_copy(
                    qg.at[dst], rs.at[me], send_sems.at[4], recv_sems.at[4],
                    device_id=where, device_id_type=MESH,
                ).start()

            return carry2

        lax.fori_loop(0, nb, send, 0)
        return carry

    lax.fori_loop(0, n_chunks, backward, 0)
    own_r = pltpu.make_async_copy(qg.at[me], rs.at[me], recv_sems.at[4])
    own_r.start()

    for p in range(pages_here):

        def page_step(c, acc):
            qc = qall[pl.ds(c * nb, nb)].reshape(cq, dim)
            return acc + jnp.dot(wbuf[c, p], qc, preferred_element_type=F32)

        pg = lax.fori_loop(0, n_chunks, page_step, jnp.zeros((slice_len, dim), F32))
        ps = pscale[p]
        pu = page_ref[p].astype(F32) * ps
        back = jnp.sum(pu * pg, axis=-1, keepdims=True)
        pagegrad_ref[p] = ((pg - pu * back) * ps).astype(BF16)

    done(hall, recv_sems.at[3])
    hallt[...] = jnp.transpose(hall[...].reshape(n * rows, hall.shape[3]))

    done(rs, recv_sems.at[4])
    sum_step = 8 if n % 8 == 0 else 1

    def add(i, acc):
        return acc + jnp.sum(rs[pl.ds(i * sum_step, sum_step)].astype(F32), axis=0)

    query_grad = lax.fori_loop(0, n // sum_step, add, jnp.zeros((rows, dim), F32))
    along = jnp.sum(query_unit * query_grad, axis=-1, keepdims=True)
    raw_grad = ((query_grad - query_unit * along) * query_scale).astype(BF16)
    rg[...] = raw_grad

    own_g = pltpu.make_async_copy(rg, rg_all.at[core, chip], recv_sems.at[5])
    own_g.start()

    def send_g(k, carry):
        dst = lax.rem(chip + k, chips)
        pltpu.make_async_remote_copy(
            rg, rg_all.at[core, chip], send_sems.at[5], recv_sems.at[5],
            device_id=(lax.div(dst, members) * pair + core, lax.rem(dst, members)), device_id_type=MESH,
        ).start()
        return carry

    lax.fori_loop(1, chips, send_g, 0)

    hgrad_ref[...] = jnp.dot(raw_grad, projt[...], preferred_element_type=F32).astype(BF16)

    done(rg_all.at[core], recv_sems.at[5])
    if pair > 1:
        pltpu.make_async_remote_copy(
            rg_all.at[core], rg_all.at[core], send_sems.at[6], recv_sems.at[6],
            device_id=(gi + 1 - 2 * core, mi), device_id_type=MESH,
        ).start()
        done(rg_all.at[1 - core], recv_sems.at[6])
    pgrad = jnp.dot(hallt[...], rg_all[...].reshape(n * rows, dim), preferred_element_type=F32)
    pgrad_ref[...] = pgrad[:hb]
    if n > 1:
        done(qall.at[pl.ds(0, n - 1)], send_sems.at[0])
        done(hsplit.at[pl.ds(0, n - 1)], send_sems.at[3])
        done(rs.at[pl.ds(0, n - 1)], send_sems.at[4])
    if members > 1:
        done(tall.at[pl.ds(0, members - 1)], send_sems.at[1])
    if groups > 1:
        done(sc_all.at[pl.ds(0, groups - 1)], send_sems.at[2])
    if chips > 1:
        done(rg_all.at[0, pl.ds(0, chips - 1)], send_sems.at[5])
    if pair > 1:
        done(rg_all.at[0], send_sems.at[6])


def finish(a_ref, b_ref, c_ref, a_out, b_out, c_out, sems):
    copies = [
        pltpu.make_async_copy(src, dst, sems.at[i])
        for i, (src, dst) in enumerate(((a_ref, a_out), (b_ref, b_out), (c_ref, c_out)))
    ]
    for copy in copies:
        copy.start()
    for copy in copies:
        copy.wait()


def body(query_hidden, projection, page_embed, page_counts, positive, hard_negs, loss_weight):
    q_here, qlen, hidden = query_hidden.shape
    pages_here, slice_len, dim = page_embed.shape
    groups = lax.axis_size("grp")
    members = lax.axis_size("dev")
    n = groups * members
    rows = q_here * qlen
    q_total = n * q_here
    nb = math.gcd(n, max(1, 256 // rows))
    n_chunks = n // nb
    cq = nb * rows
    hb = hidden // n
    hb_pad = -(-hb // 128) * 128
    pair = 2 if groups % 2 == 0 else 1
    nhn = hard_negs.shape[1]
    vmem = pl.BlockSpec(memory_space=pltpu.VMEM)
    smem = pl.BlockSpec(memory_space=pltpu.SMEM)
    hbm = pl.BlockSpec(memory_space=pltpu.HBM)
    losses, hgrad, pgrad, pagegrad = pl.pallas_call(
        functools.partial(kernel, groups, members, qlen, nhn, nb),
        out_shape=(
            jax.ShapeDtypeStruct((q_here,), F32),
            jax.ShapeDtypeStruct((rows, hidden), BF16),
            jax.ShapeDtypeStruct((hb, dim), F32),
            jax.ShapeDtypeStruct((pages_here, slice_len, dim), BF16),
        ),
        in_specs=[hbm] * 8,
        out_specs=(smem, vmem, vmem, vmem),
        scratch_shapes=[
            pltpu.VMEM((rows, dim), BF16),
            pltpu.VMEM((n, rows, dim), BF16),
            pltpu.VMEM((pages_here, slice_len, dim), BF16),
            pltpu.VMEM((pages_here, slice_len, 1), F32),
            pltpu.VMEM((n_chunks, pages_here, slice_len, cq), F32),
            pltpu.VMEM((pages_here, n * rows), F32),
            pltpu.VMEM((pages_here, n * rows), BF16),
            pltpu.VMEM((members, pages_here, n * rows), BF16),
            pltpu.VMEM((pages_here, n * rows), F32),
            pltpu.VMEM((pages_here, q_total), F32),
            pltpu.VMEM((groups, pages_here, q_total), F32),
            pltpu.VMEM((groups, pages_here, q_total), F32),
            pltpu.VMEM((n_chunks, cq, q_total), BF16),
            pltpu.VMEM((n_chunks, q_total, cq), BF16),
            pltpu.VMEM((n, rows, hb_pad), BF16),
            pltpu.VMEM((pair, n // pair, rows, hb_pad), BF16),
            pltpu.VMEM((hb_pad, n * rows), BF16),
            pltpu.VMEM((dim, hidden), BF16),
            pltpu.VMEM((n_chunks, pages_here, slice_len, cq), BF16),
            pltpu.VMEM((n, rows, dim), BF16),
            pltpu.VMEM((n, rows, dim), BF16),
            pltpu.VMEM((rows, dim), BF16),
            pltpu.VMEM((pair, n // pair, rows, dim), BF16),
            pltpu.SemaphoreType.DMA((7,)),
            pltpu.SemaphoreType.DMA((7,)),
            pltpu.VMEM((rows, hidden), BF16),
            pltpu.VMEM((hidden, dim), BF16),
            pltpu.VMEM(page_embed.shape, BF16),
            pltpu.SMEM(page_counts.shape, jnp.int32),
            pltpu.VMEM((1, page_counts.shape[0]), jnp.int32),
            pltpu.VMEM((1, q_total), jnp.int32),
            pltpu.VMEM((nhn, q_total), jnp.int32),
            pltpu.VMEM((1, q_total), F32),
            pltpu.SemaphoreType.DMA((8,)),
        ],
        compiler_params=pltpu.CompilerParams(collective_id=0, has_side_effects=True),
    )(
        query_hidden.reshape(rows, hidden),
        projection,
        page_embed,
        page_counts,
        page_counts.reshape(1, -1),
        positive.reshape(1, q_total),
        hard_negs.T,
        loss_weight.reshape(1, q_total),
    )
    hgrad, pgrad, pagegrad = pl.pallas_call(
        finish,
        out_shape=(
            jax.ShapeDtypeStruct((q_here, qlen, hidden), BF16),
            jax.ShapeDtypeStruct((hb, dim), F32),
            jax.ShapeDtypeStruct((pages_here, slice_len, dim), BF16),
        ),
        in_specs=[vmem] * 3,
        out_specs=(hbm, hbm, hbm),
        scratch_shapes=[pltpu.SemaphoreType.DMA((3,))],
    )(hgrad.reshape(q_here, qlen, hidden), pgrad, pagegrad)
    return losses, hgrad, pgrad, pagegrad


def solution(mesh):
    in_specs = (P(("grp", "dev"), None, None), P(), P("grp", "dev", None), P(), P(), P(), P())
    out_specs = (
        P(("grp", "dev")),
        P(("grp", "dev"), None, None),
        P(("grp", "dev"), None),
        P("grp", "dev", None),
    )
    return jax.shard_map(body, mesh=mesh, in_specs=in_specs, out_specs=out_specs, check_vma=False)
```

profile of v0, /device:TPU:1, one launch (start us, length us, event | category | flops | bytes accessed | tf_op | source)
XLA Modules:
  0.0 44.3 jit_solution(6285082108013955624)
XLA Ops:
  0.6 40.1 %shard_map.102 = (f32[1]{0:T(128)}, bf16[32,3584]{1,0:T(8,128)(2,1)}, f32[112,128]{1,0:T(8,128)}, bf16[4,256,128]{2,1,0:T(8,128)(2,1)}) custom-call(bf16[32,3584]{1,0:T(8,128)(2,1)} %bitcast.6, bf16[3584,128]{1,0:T(8,128)(2,1)} %proj_in.1, bf16[4,256,128]{2,1,0:T(8,128)(2,1)} %page_in.1, s32[32]{0:T(128)} %counts_in.1, s32[1,32]{1,0:T(1,128)} %bitcast.8, ...), custom_call_target="tpu_custom_call" | custom-call | tf_op jit(solution)/shard_map/pallas_call | solution.py:374
  40.7 1.9 %shard_map.103 = (bf16[1,32,3584]{2,1,0:T(8,128)(2,1)}, f32[112,128]{1,0:T(8,128)}, bf16[4,256,128]{2,1,0:T(8,128)(2,1)}) custom-call(bf16[1,32,3584]{2,1,0:T(8,128)(2,1)} %bitcast.7, f32[112,128]{1,0:T(8,128)} %get-tuple-element.13.b_ref, bf16[4,256,128]{2,1,0:T(8,128)(2,1)} %get-tuple-element.14.c_ref), custom_call_target="tpu_custom_call" | custom-call | tf_op jit(solution)/shard_map/pallas_call | solution.py:431
where the time goes:
time: 44.5 us; the launch traced here: 44.3 us
  Pallas kernels  42 us (94%)
  between operations  2.33 us (5%)
    pallas_call x1, Pallas kernels, body(): pl.pallas_call(functools.partial(kernel, groups, members, qlen, nhn, nb),...  40.1 us
    pallas_call x1, Pallas kernels, body(): pl.pallas_call(finish, out_shape=(jax.ShapeDtypeStruct((q_here, qlen, hid...  1.92 us

commit v1 on v0

v1 whole, which is shorter than its diff:
```python
import functools
import math

import jax
import jax.numpy as jnp
from jax import lax
from jax.experimental import pallas as pl
from jax.experimental.pallas import tpu as pltpu
from jax.sharding import PartitionSpec as P

SOFTMAX_HEAT = 0.02
EPSILON = 1e-06
MESH = pl.DeviceIdType.MESH
NT = (((1,), (1,)), ((), ()))
F32 = jnp.float32
BF16 = jnp.bfloat16


def split3(x):
    a = x.astype(BF16)
    r = x - a.astype(F32)
    b = r.astype(BF16)
    c = (r - b.astype(F32)).astype(BF16)
    return a, b, c


def dot3(x, ind):
    a, b, c = split3(x)
    return (
        jnp.dot(c, ind, preferred_element_type=F32)
        + jnp.dot(b, ind, preferred_element_type=F32)
        + jnp.dot(a, ind, preferred_element_type=F32)
    )


def kernel(
    groups, members, qlen, nhn, nb,
    hid_in, proj_in, page_in, counts_in, crow_in, pos_in, neg_in, lw_in,
    loss_ref, hgrad_ref, pgrad_ref, pagegrad_ref,
    qsend, qall, pn, pscale, pnt, ebuf, tot, tx, tall, totz, sgbuf, ind_down, ind_up, hsplit, hall, hallt, projt,
    wbuf, qg, rs, rg, rg_all, pgsend, pgrecv, psend, precv,
    send_sems, recv_sems, q_sems,
    hid_ref, proj_ref, page_ref, counts_ref, crow_ref, pos_ref, neg_ref, lw_ref, load_sems,
):
    loads = [
        pltpu.make_async_copy(src, dst, load_sems.at[i])
        for i, (src, dst) in enumerate(
            (
                (hid_in, hid_ref), (proj_in, proj_ref), (page_in, page_ref), (counts_in, counts_ref),
                (crow_in, crow_ref), (pos_in, pos_ref), (neg_in, neg_ref), (lw_in, lw_ref),
            )
        )
    ]
    for load in loads:
        load.start()

    n = groups * members
    pair = pn.shape[0]
    chips = n // pair
    zs = groups // pair
    rows, hidden = hid_ref.shape
    pages_here, slice_len, dim = page_ref.shape
    both = pair * pages_here
    n_chunks = chips // nb
    cq = nb * rows
    q_here = rows // qlen
    q_total = n * q_here
    hb = hidden // n
    hb_pad = hallt.shape[1]
    gi = lax.axis_index("grp")
    mi = lax.axis_index("dev")
    me = gi * members + mi
    core = lax.rem(gi, pair)
    zi = lax.div(gi, pair)
    chip = zi * members + mi
    my_chunk = lax.div(chip, nb)
    partner = (gi + 1 - 2 * core, mi)

    def place(dst):
        return (lax.div(dst, members) * pair + core, lax.rem(dst, members))

    barrier = pltpu.get_barrier_semaphore()

    def greet(k, carry):
        where = place(lax.rem(chip + k, chips))
        pl.semaphore_signal(barrier, inc=1, device_id=where, device_id_type=MESH)
        return carry

    lax.fori_loop(1, chips, greet, 0)
    if pair > 1:
        pl.semaphore_signal(barrier, inc=1, device_id=partner, device_id_type=MESH)

    def done(ref, sem):
        pltpu.make_async_copy(ref, ref, sem).wait()

    def to_plane(src, dst, send_sem, recv_sem):
        def send(k, carry):
            where = place(lax.rem(chip + k, chips))
            pltpu.make_async_remote_copy(
                src, dst, send_sem, recv_sem, device_id=where, device_id_type=MESH
            ).start()
            return carry

        lax.fori_loop(1, chips, send, 0)

    def to_partner(src, dst, i):
        pltpu.make_async_remote_copy(
            src, dst, send_sems.at[i], recv_sems.at[i], device_id=partner, device_id_type=MESH
        ).start()

    loads[0].wait()
    loads[1].wait()
    query_raw = jnp.dot(hid_ref[...], proj_ref[...], preferred_element_type=F32)
    query_scale = lax.rsqrt(jnp.sum(query_raw * query_raw, axis=-1, keepdims=True) + EPSILON)
    query_unit = query_raw * query_scale
    qsend[...] = query_unit.astype(BF16)

    pl.semaphore_wait(barrier, chips - 1 + pair - 1)

    pltpu.make_async_copy(qsend, qall.at[chip], q_sems.at[my_chunk]).start()
    to_plane(qsend, qall.at[chip], send_sems.at[0], q_sems.at[my_chunk])

    loads[2].wait()
    for p in range(pages_here):
        praw = page_ref[p].astype(F32)
        ps = lax.rsqrt(jnp.sum(praw * praw, axis=-1, keepdims=True) + EPSILON)
        pscale[p] = ps
        pn[core, p] = (praw * ps).astype(BF16)
    if pair > 1:
        to_partner(pn.at[core], pn.at[core], 6)

    for j in range(chips):
        zj, mj = divmod(j, members)
        for h in range(pair):
            d = (zj * pair + h) * members + mj
            hsplit[j, :, h * hb_pad : h * hb_pad + hb] = hid_ref[:, d * hb : (d + 1) * hb]
            if hb_pad > hb:
                hsplit[j, :, h * hb_pad + hb : (h + 1) * hb_pad] = jnp.zeros((rows, hb_pad - hb), BF16)
    pltpu.make_async_copy(hsplit.at[chip], hall.at[chip], recv_sems.at[3]).start()

    def send_h(k, carry):
        dst = lax.rem(chip + k, chips)
        pltpu.make_async_remote_copy(
            hsplit.at[dst], hall.at[chip], send_sems.at[3], recv_sems.at[3],
            device_id=place(dst), device_id_type=MESH,
        ).start()
        return carry

    lax.fori_loop(1, chips, send_h, 0)

    projt[...] = jnp.transpose(proj_ref[...])

    q_row = lax.broadcasted_iota(jnp.int32, (1, q_total), 1)
    q_col = lax.broadcasted_iota(jnp.int32, (q_total, 1), 0)

    def first_token(q):
        dev = lax.div(q, q_here)
        grp = lax.div(dev, members)
        at = (lax.div(grp, pair) * members + lax.rem(dev, members)) * rows + lax.rem(q, q_here) * qlen
        return jnp.where(lax.rem(grp, pair) == core, at, -qlen)

    row_start = first_token(q_row)
    col_start = first_token(q_col)

    def indicators(c, carry):
        r = lax.broadcasted_iota(jnp.int32, (cq, q_total), 0) + c * cq
        ind_down[c] = jnp.where((r >= row_start) & (r < row_start + qlen), 1.0, 0.0).astype(BF16)
        r = lax.broadcasted_iota(jnp.int32, (q_total, cq), 1) + c * cq
        ind_up[c] = jnp.where((r >= col_start) & (r < col_start + qlen), 1.0, 0.0).astype(BF16)
        return carry

    lax.fori_loop(0, n_chunks, indicators, 0)

    for load in loads[3:]:
        load.wait()
    token = lax.broadcasted_iota(jnp.int32, (slice_len, 1), 0) + mi * slice_len
    biases = []
    for p in range(both):
        count = counts_ref[zi * both + p]
        biases.append(jnp.where(token < count, 0.0, -1e30).astype(F32))

    page_total = groups * pages_here
    pos_row = pos_ref[...].astype(F32)
    neg_rows = [neg_ref[j : j + 1, :].astype(F32) for j in range(nhn)]
    lw_row = lw_ref[...]
    eye = lax.broadcasted_iota(jnp.int32, (page_total, page_total), 0) == lax.broadcasted_iota(
        jnp.int32, (page_total, page_total), 1
    )
    count_col = jnp.sum(jnp.where(eye, crow_ref[...].astype(F32), 0.0), axis=1, keepdims=True)
    log_count = (SOFTMAX_HEAT * qlen) * jnp.log(count_col)
    page_id = lax.broadcasted_iota(jnp.int32, (page_total, q_total), 0).astype(F32)
    pos_hot = jnp.where(page_id == pos_row, 1.0, 0.0)
    neg_hots = [jnp.where(page_id == row, 1.0, 0.0) for row in neg_rows]

    if pair > 1:
        done(pn.at[1 - core], recv_sems.at[6])

    def forward(i, carry):
        c = lax.rem(my_chunk + i, n_chunks)
        done(qall.at[pl.ds(0, nb)], q_sems.at[c])
        qc = qall[pl.ds(c * nb, nb)].reshape(cq, dim)
        parts = []
        for p in range(both):
            s = lax.dot_general(pn[p // pages_here, p % pages_here], qc, NT, preferred_element_type=F32)
            e = jnp.exp(s * (1.0 / SOFTMAX_HEAT) + biases[p])
            ebuf[c, p] = e
            parts.append(jnp.sum(e, axis=0, keepdims=True))
        tot[c] = jnp.concatenate(parts, axis=0)
        return carry

    lax.fori_loop(0, n_chunks, forward, 0)

    tx[...] = tot[...].reshape(n_chunks * both, cq).astype(BF16)
    pltpu.make_async_copy(tx, tall.at[chip], recv_sems.at[1]).start()
    to_plane(tx, tall.at[chip], send_sems.at[1], recv_sems.at[1])

    pnt[...] = jnp.transpose(pn[...].reshape(both * slice_len, dim))

    done(tall, recv_sems.at[1])

    for z in range(zs):

        def add_slices(m, acc):
            return acc + tall[z * members + m].astype(F32)

        if members <= 4:
            total = tall[z * members].astype(F32)
            for m in range(1, members):
                total = add_slices(m, total)
        else:
            total = lax.fori_loop(0, members, add_slices, jnp.zeros((n_chunks * both, cq), F32))
        totz[z] = total.reshape(n_chunks, both, cq)

    def compress(c, acc):
        return acc + dot3(jnp.log(totz[:, c].reshape(zs * both, cq)), ind_down[c])

    acc = jnp.zeros((page_total, q_total), F32)
    if n_chunks <= 4:
        for c in range(n_chunks):
            acc = compress(c, acc)
    else:
        acc = lax.fori_loop(0, n_chunks, compress, acc)
    scores = SOFTMAX_HEAT * acc - log_count

    log_total = jnp.log(jnp.sum(jnp.exp(scores), axis=0, keepdims=True))
    pos_score = jnp.sum(scores * pos_hot, axis=0, keepdims=True)
    soft = jnp.zeros((1, q_total), F32)
    push = jnp.zeros((page_total, q_total), F32)
    for j in range(nhn):
        margin = jnp.sum(scores * neg_hots[j], axis=0, keepdims=True) - pos_score
        small = jnp.exp(-jnp.abs(margin))
        soft = soft + jnp.maximum(margin, 0.0) + jnp.log1p(small)
        sig = jnp.where(margin >= 0, 1.0, small) / (1.0 + small)
        push = push + sig * (neg_hots[j] - pos_hot)
    losses = log_total - pos_score + soft / nhn
    grads = lw_row * (jnp.exp(scores - log_total) - pos_hot + push / nhn)
    for z in range(zs):
        sgbuf[z] = grads[z * both : (z + 1) * both, :]
    score_grad = sgbuf[zi]
    grad3 = split3(score_grad)

    def backward(i, carry):
        c = lax.rem(my_chunk + 1 + i, n_chunks)
        ind = ind_up[c]
        wide = (
            jnp.dot(grad3[2], ind, preferred_element_type=F32)
            + jnp.dot(grad3[1], ind, preferred_element_type=F32)
            + jnp.dot(grad3[0], ind, preferred_element_type=F32)
        )
        factor = wide / totz[zi, c]
        for p in range(both):
            wbuf[c, p] = (ebuf[c, p] * factor[p : p + 1, :]).astype(BF16)
        w = wbuf[c].reshape(both * slice_len, cq)
        gt = jnp.dot(pnt[...], w, preferred_element_type=F32)
        qg[pl.ds(c * nb, nb)] = jnp.transpose(gt).astype(BF16).reshape(nb, rows, dim)

        def send(k, carry2):
            dst = c * nb + k

            @pl.when(dst != chip)
            def _():
                pltpu.make_async_remote_copy(
                    qg.at[dst], rs.at[chip], send_sems.at[4], recv_sems.at[4],
                    device_id=place(dst), device_id_type=MESH,
                ).start()

            return carry2

        lax.fori_loop(0, nb, send, 0)
        return carry

    lax.fori_loop(0, n_chunks, backward, 0)
    pltpu.make_async_copy(qg.at[chip], rs.at[chip], recv_sems.at[4]).start()

    lane = lax.broadcasted_iota(jnp.int32, (1, q_total), 1)
    for i in range(q_here):
        loss_ref[i] = jnp.sum(jnp.where(lane == me * q_here + i, losses, 0.0))

    def page_grad(half, p):
        def page_step(c, acc):
            qc = qall[pl.ds(c * nb, nb)].reshape(cq, dim)
            return acc + jnp.dot(wbuf[c, half * pages_here + p], qc, preferred_element_type=F32)

        acc = jnp.zeros((slice_len, dim), F32)
        if n_chunks <= 4:
            for c in range(n_chunks):
                acc = page_step(c, acc)
            return acc
        return lax.fori_loop(0, n_chunks, page_step, acc)

    if pair > 1:
        for p in range(pages_here):
            pgsend[p] = page_grad(1 - core, p).astype(BF16)
        to_partner(pgsend, pgrecv, 7)

    done(hall, recv_sems.at[3])
    for h in range(pair):
        hallt[h] = jnp.transpose(hall[:, :, h * hb_pad : (h + 1) * hb_pad].reshape(chips * rows, hb_pad))

    own_grads = [page_grad(core, p) for p in range(pages_here)]
    if pair > 1:
        done(pgrecv, recv_sems.at[7])
    for p in range(pages_here):
        pg = own_grads[p]
        if pair > 1:
            pg = pg + pgrecv[p].astype(F32)
        ps = pscale[p]
        pu = page_ref[p].astype(F32) * ps
        back = jnp.sum(pu * pg, axis=-1, keepdims=True)
        pagegrad_ref[p] = ((pg - pu * back) * ps).astype(BF16)

    done(rs, recv_sems.at[4])
    sum_step = 8 if chips % 8 == 0 else 1

    def add(i, acc):
        return acc + jnp.sum(rs[pl.ds(i * sum_step, sum_step)].astype(F32), axis=0)

    query_grad = lax.fori_loop(0, chips // sum_step, add, jnp.zeros((rows, dim), F32))
    along = jnp.sum(query_unit * query_grad, axis=-1, keepdims=True)
    raw_grad = ((query_grad - query_unit * along) * query_scale).astype(BF16)
    rg[...] = raw_grad

    pltpu.make_async_copy(rg, rg_all.at[chip], recv_sems.at[5]).start()
    to_plane(rg, rg_all.at[chip], send_sems.at[5], recv_sems.at[5])

    hgrad_ref[...] = jnp.dot(raw_grad, projt[...], preferred_element_type=F32).astype(BF16)

    done(rg_all, recv_sems.at[5])
    rga = rg_all[...].reshape(chips * rows, dim)
    if pair > 1:
        psend[...] = jnp.dot(hallt[1 - core], rga, preferred_element_type=F32)
        to_partner(psend, precv, 8)
    pgrad = jnp.dot(hallt[core], rga, preferred_element_type=F32)
    if pair > 1:
        done(precv, recv_sems.at[8])
        pgrad = pgrad + precv[...]
    pgrad_ref[...] = pgrad[:hb]
    if chips > 1:
        done(qall.at[pl.ds(0, chips - 1)], send_sems.at[0])
        done(hsplit.at[pl.ds(0, chips - 1)], send_sems.at[3])
        done(rs.at[pl.ds(0, chips - 1)], send_sems.at[4])
        done(tall.at[pl.ds(0, chips - 1)], send_sems.at[1])
        done(rg_all.at[pl.ds(0, chips - 1)], send_sems.at[5])
    if pair > 1:
        done(pn.at[0], send_sems.at[6])
        done(pgsend, send_sems.at[7])
        done(psend, send_sems.at[8])


def finish(a_ref, b_ref, c_ref, a_out, b_out, c_out, sems):
    copies = [
        pltpu.make_async_copy(src, dst, sems.at[i])
        for i, (src, dst) in enumerate(((a_ref, a_out), (b_ref, b_out), (c_ref, c_out)))
    ]
    for copy in copies:
        copy.start()
    for copy in copies:
        copy.wait()


def body(query_hidden, projection, page_embed, page_counts, positive, hard_negs, loss_weight):
    q_here, qlen, hidden = query_hidden.shape
    pages_here, slice_len, dim = page_embed.shape
    groups = lax.axis_size("grp")
    members = lax.axis_size("dev")
    n = groups * members
    rows = q_here * qlen
    q_total = n * q_here
    pair = 2 if groups % 2 == 0 else 1
    chips = n // pair
    zs = groups // pair
    both = pair * pages_here
    nb = math.gcd(chips, max(1, 256 // rows))
    n_chunks = chips // nb
    cq = nb * rows
    hb = hidden // n
    hb_pad = -(-hb // 128) * 128
    nhn = hard_negs.shape[1]
    vmem = pl.BlockSpec(memory_space=pltpu.VMEM)
    smem = pl.BlockSpec(memory_space=pltpu.SMEM)
    hbm = pl.BlockSpec(memory_space=pltpu.HBM)
    losses, hgrad, pgrad, pagegrad = pl.pallas_call(
        functools.partial(kernel, groups, members, qlen, nhn, nb),
        out_shape=(
            jax.ShapeDtypeStruct((q_here,), F32),
            jax.ShapeDtypeStruct((rows, hidden), BF16),
            jax.ShapeDtypeStruct((hb, dim), F32),
            jax.ShapeDtypeStruct((pages_here, slice_len, dim), BF16),
        ),
        in_specs=[hbm] * 8,
        out_specs=(smem, vmem, vmem, vmem),
        scratch_shapes=[
            pltpu.VMEM((rows, dim), BF16),
            pltpu.VMEM((chips, rows, dim), BF16),
            pltpu.VMEM((pair, pages_here, slice_len, dim), BF16),
            pltpu.VMEM((pages_here, slice_len, 1), F32),
            pltpu.VMEM((dim, both * slice_len), BF16),
            pltpu.VMEM((n_chunks, both, slice_len, cq), F32),
            pltpu.VMEM((n_chunks, both, cq), F32),
            pltpu.VMEM((n_chunks * both, cq), BF16),
            pltpu.VMEM((chips, n_chunks * both, cq), BF16),
            pltpu.VMEM((zs, n_chunks, both, cq), F32),
            pltpu.VMEM((zs, both, q_total), F32),
            pltpu.VMEM((n_chunks, cq, q_total), BF16),
            pltpu.VMEM((n_chunks, q_total, cq), BF16),
            pltpu.VMEM((chips, rows, pair * hb_pad), BF16),
            pltpu.VMEM((chips, rows, pair * hb_pad), BF16),
            pltpu.VMEM((pair, hb_pad, chips * rows), BF16),
            pltpu.VMEM((dim, hidden), BF16),
            pltpu.VMEM((n_chunks, both, slice_len, cq), BF16),
            pltpu.VMEM((chips, rows, dim), BF16),
            pltpu.VMEM((chips, rows, dim), BF16),
            pltpu.VMEM((rows, dim), BF16),
            pltpu.VMEM((chips, rows, dim), BF16),
            pltpu.VMEM((pages_here, slice_len, dim), BF16),
            pltpu.VMEM((pages_here, slice_len, dim), BF16),
            pltpu.VMEM((hb_pad, dim), F32),
            pltpu.VMEM((hb_pad, dim), F32),
            pltpu.SemaphoreType.DMA((9,)),
            pltpu.SemaphoreType.DMA((9,)),
            pltpu.SemaphoreType.DMA((n_chunks,)),
            pltpu.VMEM((rows, hidden), BF16),
            pltpu.VMEM((hidden, dim), BF16),
            pltpu.VMEM(page_embed.shape, BF16),
            pltpu.SMEM(page_counts.shape, jnp.int32),
            pltpu.VMEM((1, page_counts.shape[0]), jnp.int32),
            pltpu.VMEM((1, q_total), jnp.int32),
            pltpu.VMEM((nhn, q_total), jnp.int32),
            pltpu.VMEM((1, q_total), F32),
            pltpu.SemaphoreType.DMA((8,)),
        ],
        compiler_params=pltpu.CompilerParams(collective_id=0, has_side_effects=True),
    )(
        query_hidden.reshape(rows, hidden),
        projection,
        page_embed,
        page_counts,
        page_counts.reshape(1, -1),
        positive.reshape(1, q_total),
        hard_negs.T,
        loss_weight.reshape(1, q_total),
    )
    hgrad, pgrad, pagegrad = pl.pallas_call(
        finish,
        out_shape=(
            jax.ShapeDtypeStruct((q_here, qlen, hidden), BF16),
            jax.ShapeDtypeStruct((hb, dim), F32),
            jax.ShapeDtypeStruct((pages_here, slice_len, dim), BF16),
        ),
        in_specs=[vmem] * 3,
        out_specs=(hbm, hbm, hbm),
        scratch_shapes=[pltpu.SemaphoreType.DMA((3,))],
    )(hgrad.reshape(q_here, qlen, hidden), pgrad, pagegrad)
    return losses, hgrad, pgrad, pagegrad


def solution(mesh):
    in_specs = (P(("grp", "dev"), None, None), P(), P("grp", "dev", None), P(), P(), P(), P())
    out_specs = (
        P(("grp", "dev")),
        P(("grp", "dev"), None, None),
        P(("grp", "dev"), None),
        P("grp", "dev", None),
    )
    return jax.shard_map(body, mesh=mesh, in_specs=in_specs, out_specs=out_specs, check_vma=False)
```

time: 44.5 us -> 36.6 us (0.82)
  Pallas kernels: 42 us -> 34.1 us
    pallas_call x1, Pallas kernels: 40.1 us -> 32.2 us  [body(): pl.pallas_call(functools.partial(kernel, groups, members, qlen, nhn, nb),...]
where the time goes in v1:
time: 36.6 us; the launch traced here: 36.4 us
  Pallas kernels  34.1 us (93%)
  between operations  2.33 us (6%)
    pallas_call x1, Pallas kernels, body(): pl.pallas_call(functools.partial(kernel, groups, members, qlen, nhn, nb),...  32.2 us
    pallas_call x1, Pallas kernels, body(): pl.pallas_call(finish, out_shape=(jax.ShapeDtypeStruct((q_here, qlen, hid...  1.92 us

profile of v1, /device:TPU:1, one launch (start us, length us, event | category | flops | bytes accessed | tf_op | source)
XLA Modules:
  0.0 36.4 jit_solution(6222440474835261187)
XLA Ops:
  0.6 32.2 %shard_map.102 = (f32[1]{0:T(128)}, bf16[32,3584]{1,0:T(8,128)(2,1)}, f32[112,128]{1,0:T(8,128)}, bf16[4,256,128]{2,1,0:T(8,128)(2,1)}) custom-call(bf16[32,3584]{1,0:T(8,128)(2,1)} %bitcast.6, bf16[3584,128]{1,0:T(8,128)(2,1)} %proj_in.1, bf16[4,256,128]{2,1,0:T(8,128)(2,1)} %page_in.1, s32[32]{0:T(128)} %counts_in.1, s32[1,32]{1,0:T(1,128)} %bitcast.8, ...), custom_call_target="tpu_custom_call" | custom-call | tf_op jit(solution)/shard_map/pallas_call | solution.py:402
  32.8 1.9 %shard_map.103 = (bf16[1,32,3584]{2,1,0:T(8,128)(2,1)}, f32[112,128]{1,0:T(8,128)}, bf16[4,256,128]{2,1,0:T(8,128)(2,1)}) custom-call(bf16[1,32,3584]{2,1,0:T(8,128)(2,1)} %bitcast.7, f32[112,128]{1,0:T(8,128)} %get-tuple-element.13.b_ref, bf16[4,256,128]{2,1,0:T(8,128)(2,1)} %get-tuple-element.14.c_ref), custom_call_target="tpu_custom_call" | custom-call | tf_op jit(solution)/shard_map/pallas_call | solution.py:463

commit v2 on v1

--- a/solution.py
+++ b/solution.py
@@ -51,9 +51,6 @@
             )
         )
     ]
-    for load in loads:
-        load.start()
-
     n = groups * members
     pair = pn.shape[0]
     chips = n // pair
@@ -90,6 +87,9 @@
     if pair > 1:
         pl.semaphore_signal(barrier, inc=1, device_id=partner, device_id_type=MESH)
 
+    for load in loads:
+        load.start()
+
     def done(ref, sem):
         pltpu.make_async_copy(ref, ref, sem).wait()
 
@@ -146,7 +146,8 @@
         ).start()
         return carry
 
-    lax.fori_loop(1, chips, send_h, 0)
+    cut_a, cut_b = 1 + (chips - 1) // 3, 1 + 2 * (chips - 1) // 3
+    lax.fori_loop(1, cut_a, send_h, 0)
 
     projt[...] = jnp.transpose(proj_ref[...])
 
@@ -202,7 +203,7 @@
         parts = []
         for p in range(both):
             s = lax.dot_general(pn[p // pages_here, p % pages_here], qc, NT, preferred_element_type=F32)
-            e = jnp.exp(s * (1.0 / SOFTMAX_HEAT) + biases[p])
+            e = jnp.exp2(s * (math.log2(math.e) / SOFTMAX_HEAT) + biases[p])
             ebuf[c, p] = e
             parts.append(jnp.sum(e, axis=0, keepdims=True))
         tot[c] = jnp.concatenate(parts, axis=0)
@@ -213,6 +214,7 @@
     tx[...] = tot[...].reshape(n_chunks * both, cq).astype(BF16)
     pltpu.make_async_copy(tx, tall.at[chip], recv_sems.at[1]).start()
     to_plane(tx, tall.at[chip], send_sems.at[1], recv_sems.at[1])
+    lax.fori_loop(cut_a, cut_b, send_h, 0)
 
     pnt[...] = jnp.transpose(pn[...].reshape(both * slice_len, dim))
 
@@ -291,10 +293,15 @@
 
     lax.fori_loop(0, n_chunks, backward, 0)
     pltpu.make_async_copy(qg.at[chip], rs.at[chip], recv_sems.at[4]).start()
+    lax.fori_loop(cut_b, chips, send_h, 0)
 
     lane = lax.broadcasted_iota(jnp.int32, (1, q_total), 1)
+    own = lax.broadcasted_iota(jnp.int32, (1, q_here), 1)
+    mine = jnp.zeros((1, q_here), F32)
     for i in range(q_here):
-        loss_ref[i] = jnp.sum(jnp.where(lane == me * q_here + i, losses, 0.0))
+        one = jnp.sum(jnp.where(lane == me * q_here + i, losses, 0.0), axis=1, keepdims=True)
+        mine = jnp.where(own == i, one, mine)
+    loss_ref[...] = mine
 
     def page_grad(half, p):
         def page_step(c, acc):
@@ -313,9 +320,19 @@
             pgsend[p] = page_grad(1 - core, p).astype(BF16)
         to_partner(pgsend, pgrecv, 7)
 
-    done(hall, recv_sems.at[3])
-    for h in range(pair):
-        hallt[h] = jnp.transpose(hall[:, :, h * hb_pad : (h + 1) * hb_pad].reshape(chips * rows, hb_pad))
+    done(rs, recv_sems.at[4])
+    sum_step = 8 if chips % 8 == 0 else 1
+
+    def add(i, acc):
+        return acc + jnp.sum(rs[pl.ds(i * sum_step, sum_step)].astype(F32), axis=0)
+
+    query_grad = lax.fori_loop(0, chips // sum_step, add, jnp.zeros((rows, dim), F32))
+    along = jnp.sum(query_unit * query_grad, axis=-1, keepdims=True)
+    raw_grad = ((query_grad - query_unit * along) * query_scale).astype(BF16)
+    rg[...] = raw_grad
+
+    pltpu.make_async_copy(rg, rg_all.at[chip], recv_sems.at[5]).start()
+    to_plane(rg, rg_all.at[chip], send_sems.at[5], recv_sems.at[5])
 
     own_grads = [page_grad(core, p) for p in range(pages_here)]
     if pair > 1:
@@ -329,21 +346,11 @@
         back = jnp.sum(pu * pg, axis=-1, keepdims=True)
         pagegrad_ref[p] = ((pg - pu * back) * ps).astype(BF16)
 
-    done(rs, recv_sems.at[4])
-    sum_step = 8 if chips % 8 == 0 else 1
-
-    def add(i, acc):
-        return acc + jnp.sum(rs[pl.ds(i * sum_step, sum_step)].astype(F32), axis=0)
-
-    query_grad = lax.fori_loop(0, chips // sum_step, add, jnp.zeros((rows, dim), F32))
-    along = jnp.sum(query_unit * query_grad, axis=-1, keepdims=True)
-    raw_grad = ((query_grad - query_unit * along) * query_scale).astype(BF16)
-    rg[...] = raw_grad
-
-    pltpu.make_async_copy(rg, rg_all.at[chip], recv_sems.at[5]).start()
-    to_plane(rg, rg_all.at[chip], send_sems.at[5], recv_sems.at[5])
-
     hgrad_ref[...] = jnp.dot(raw_grad, projt[...], preferred_element_type=F32).astype(BF16)
+
+    done(hall, recv_sems.at[3])
+    for h in range(pair):
+        hallt[h] = jnp.transpose(hall[:, :, h * hb_pad : (h + 1) * hb_pad].reshape(chips * rows, hb_pad))
 
     done(rg_all, recv_sems.at[5])
     rga = rg_all[...].reshape(chips * rows, dim)
@@ -367,10 +374,10 @@
         done(psend, send_sems.at[8])
 
 
-def finish(a_ref, b_ref, c_ref, a_out, b_out, c_out, sems):
+def finish(a_ref, b_ref, c_ref, d_ref, a_out, b_out, c_out, d_out, sems):
     copies = [
         pltpu.make_async_copy(src, dst, sems.at[i])
-        for i, (src, dst) in enumerate(((a_ref, a_out), (b_ref, b_out), (c_ref, c_out)))
+        for i, (src, dst) in enumerate(((d_ref, d_out), (b_ref, b_out), (a_ref, a_out), (c_ref, c_out)))
     ]
     for copy in copies:
         copy.start()
@@ -402,13 +409,13 @@
     losses, hgrad, pgrad, pagegrad = pl.pallas_call(
         functools.partial(kernel, groups, members, qlen, nhn, nb),
         out_shape=(
-            jax.ShapeDtypeStruct((q_here,), F32),
+            jax.ShapeDtypeStruct((1, q_here), F32),
             jax.ShapeDtypeStruct((rows, hidden), BF16),
             jax.ShapeDtypeStruct((hb, dim), F32),
             jax.ShapeDtypeStruct((pages_here, slice_len, dim), BF16),
         ),
         in_specs=[hbm] * 8,
-        out_specs=(smem, vmem, vmem, vmem),
+        out_specs=(vmem, vmem, vmem, vmem),
         scratch_shapes=[
             pltpu.VMEM((rows, dim), BF16),
             pltpu.VMEM((chips, rows, dim), BF16),
@@ -460,18 +467,19 @@
         hard_negs.T,
         loss_weight.reshape(1, q_total),
     )
-    hgrad, pgrad, pagegrad = pl.pallas_call(
+    hgrad, pgrad, pagegrad, losses = pl.pallas_call(
         finish,
         out_shape=(
             jax.ShapeDtypeStruct((q_here, qlen, hidden), BF16),
             jax.ShapeDtypeStruct((hb, dim), F32),
             jax.ShapeDtypeStruct((pages_here, slice_len, dim), BF16),
+            jax.ShapeDtypeStruct((1, q_here), F32),
         ),
-        in_specs=[vmem] * 3,
-        out_specs=(hbm, hbm, hbm),
-        scratch_shapes=[pltpu.SemaphoreType.DMA((3,))],
-    )(hgrad.reshape(q_here, qlen, hidden), pgrad, pagegrad)
-    return losses, hgrad, pgrad, pagegrad
+        in_specs=[vmem, vmem, vmem, vmem],
+        out_specs=(hbm, hbm, hbm, hbm),
+        scratch_shapes=[pltpu.SemaphoreType.DMA((4,))],
+    )(hgrad.reshape(q_here, qlen, hidden), pgrad, pagegrad, losses)
+    return losses.reshape(q_here), hgrad, pgrad, pagegrad
 
 
 def solution(mesh):

time: 36.6 us -> 34 us (0.929)
  between operations: 2.33 us -> 0.64 us
  Pallas kernels: 34.1 us -> 33.2 us
    pallas_call x1, Pallas kernels: 32.2 us -> 30.7 us  [body(): pl.pallas_call(functools.partial(kernel, groups, members, qlen, nhn, nb),...]
    pallas_call x1, Pallas kernels: 1.92 us -> 2.49 us  [body(): pl.pallas_call(finish, out_shape=(jax.ShapeDtypeStruct((q_here, qlen, hid...]
where the time goes in v2:
time: 34 us; the launch traced here: 33.8 us
  Pallas kernels  33.2 us (98%)
  between operations  0.64 us (2%)
    pallas_call x1, Pallas kernels, body(): pl.pallas_call(functools.partial(kernel, groups, members, qlen, nhn, nb),...  30.7 us
    pallas_call x1, Pallas kernels, body(): pl.pallas_call(finish, out_shape=(jax.ShapeDtypeStruct((q_here, qlen, hid...  2.49 us

profile of v2, /device:TPU:1, one launch (start us, length us, event | category | flops | bytes accessed | tf_op | source)
XLA Modules:
  0.0 33.8 jit_solution(15423165089685337930)
XLA Ops:
  0.6 30.7 %shard_map.102 = (f32[1,1]{1,0:T(1,128)}, bf16[32,3584]{1,0:T(8,128)(2,1)}, f32[112,128]{1,0:T(8,128)}, bf16[4,256,128]{2,1,0:T(8,128)(2,1)}) custom-call(bf16[32,3584]{1,0:T(8,128)(2,1)} %bitcast.7, bf16[3584,128]{1,0:T(8,128)(2,1)} %proj_in.1, bf16[4,256,128]{2,1,0:T(8,128)(2,1)} %page_in.1, s32[32]{0:T(128)} %counts_in.1, s32[1,32]{1,0:T(1,128)} %bitcast.9, ...), custom_call_target="tpu_custom_call" | custom-call | tf_op jit(solution)/shard_map/pallas_call | solution.py:409
  31.3 2.5 %shard_map.103 = (bf16[1,32,3584]{2,1,0:T(8,128)(2,1)}, f32[112,128]{1,0:T(8,128)}, bf16[4,256,128]{2,1,0:T(8,128)(2,1)}, f32[1,1]{1,0:T(1,128)}) custom-call(bf16[1,32,3584]{2,1,0:T(8,128)(2,1)} %bitcast.8, f32[112,128]{1,0:T(8,128)} %get-tuple-element.13.b_ref, bf16[4,256,128]{2,1,0:T(8,128)(2,1)} %get-tuple-element.14.c_ref, f32[1,1]{1,0:T(1,128)} %get-tuple-element.15.d_ref), custom_call_target="tpu_custom_call" | custom-call | tf_op jit(solution)/shard_map/pallas_call | solution.py:470

commit v3 on v2

--- a/solution.py
+++ b/solution.py
@@ -36,11 +36,12 @@
 def kernel(
     groups, members, qlen, nhn, nb,
     hid_in, proj_in, page_in, counts_in, crow_in, pos_in, neg_in, lw_in,
-    loss_ref, hgrad_ref, pgrad_ref, pagegrad_ref,
+    loss_out, hgrad_out, pgrad_ref, pagegrad_out,
     qsend, qall, pn, pscale, pnt, ebuf, tot, tx, tall, totz, sgbuf, ind_down, ind_up, hsplit, hall, hallt, projt,
     wbuf, qg, rs, rg, rg_all, pgsend, pgrecv, psend, precv,
     send_sems, recv_sems, q_sems,
     hid_ref, proj_ref, page_ref, counts_ref, crow_ref, pos_ref, neg_ref, lw_ref, load_sems,
+    loss_ref, hgrad_ref, pagegrad_ref, out_sems,
 ):
     loads = [
         pltpu.make_async_copy(src, dst, load_sems.at[i])
@@ -302,6 +303,8 @@
         one = jnp.sum(jnp.where(lane == me * q_here + i, losses, 0.0), axis=1, keepdims=True)
         mine = jnp.where(own == i, one, mine)
     loss_ref[...] = mine
+    store_loss = pltpu.make_async_copy(loss_ref, loss_out, out_sems.at[0])
+    store_loss.start()
 
     def page_grad(half, p):
         def page_step(c, acc):
@@ -345,8 +348,12 @@
         pu = page_ref[p].astype(F32) * ps
         back = jnp.sum(pu * pg, axis=-1, keepdims=True)
         pagegrad_ref[p] = ((pg - pu * back) * ps).astype(BF16)
+    store_pages = pltpu.make_async_copy(pagegrad_ref, pagegrad_out, out_sems.at[1])
+    store_pages.start()
 
     hgrad_ref[...] = jnp.dot(raw_grad, projt[...], preferred_element_type=F32).astype(BF16)
+    store_hidden = pltpu.make_async_copy(hgrad_ref, hgrad_out, out_sems.at[2])
+    store_hidden.start()
 
     done(hall, recv_sems.at[3])
     for h in range(pair):
@@ -362,6 +369,9 @@
         done(precv, recv_sems.at[8])
         pgrad = pgrad + precv[...]
     pgrad_ref[...] = pgrad[:hb]
+    store_loss.wait()
+    store_pages.wait()
+    store_hidden.wait()
     if chips > 1:
         done(qall.at[pl.ds(0, chips - 1)], send_sems.at[0])
         done(hsplit.at[pl.ds(0, chips - 1)], send_sems.at[3])
@@ -374,15 +384,17 @@
         done(psend, send_sems.at[8])
 
 
-def finish(a_ref, b_ref, c_ref, d_ref, a_out, b_out, c_out, d_out, sems):
-    copies = [
-        pltpu.make_async_copy(src, dst, sems.at[i])
-        for i, (src, dst) in enumerate(((d_ref, d_out), (b_ref, b_out), (a_ref, a_out), (c_ref, c_out)))
-    ]
-    for copy in copies:
-        copy.start()
-    for copy in copies:
-        copy.wait()
+def finish(a_in, b_in, c_in, d_in, a_out, b_out, c_out, d_out, a_buf, b_buf, c_buf, d_buf, in_sems, out_sems):
+    moves = ((b_in, b_buf, b_out), (d_in, d_buf, d_out), (a_in, a_buf, a_out), (c_in, c_buf, c_out))
+    loads = [pltpu.make_async_copy(src, buf, in_sems.at[i]) for i, (src, buf, _) in enumerate(moves)]
+    stores = [pltpu.make_async_copy(buf, dst, out_sems.at[i]) for i, (_, buf, dst) in enumerate(moves)]
+    for load in loads:
+        load.start()
+    for load, store in zip(loads, stores, strict=True):
+        load.wait()
+        store.start()
+    for store in stores:
+        store.wait()
 
 
 def body(query_hidden, projection, page_embed, page_counts, positive, hard_negs, loss_weight):
@@ -415,7 +427,7 @@
             jax.ShapeDtypeStruct((pages_here, slice_len, dim), BF16),
         ),
         in_specs=[hbm] * 8,
-        out_specs=(vmem, vmem, vmem, vmem),
+        out_specs=(hbm, hbm, vmem, hbm),
         scratch_shapes=[
             pltpu.VMEM((rows, dim), BF16),
             pltpu.VMEM((chips, rows, dim), BF16),
@@ -455,6 +467,10 @@
             pltpu.VMEM((nhn, q_total), jnp.int32),
             pltpu.VMEM((1, q_total), F32),
             pltpu.SemaphoreType.DMA((8,)),
+            pltpu.VMEM((1, q_here), F32),
+            pltpu.VMEM((rows, hidden), BF16),
+            pltpu.VMEM(page_embed.shape, BF16),
+            pltpu.SemaphoreType.DMA((3,)),
         ],
         compiler_params=pltpu.CompilerParams(collective_id=0, has_side_effects=True),
     )(
@@ -475,9 +491,16 @@
             jax.ShapeDtypeStruct((pages_here, slice_len, dim), BF16),
             jax.ShapeDtypeStruct((1, q_here), F32),
         ),
-        in_specs=[vmem, vmem, vmem, vmem],
+        in_specs=[hbm] * 4,
         out_specs=(hbm, hbm, hbm, hbm),
-        scratch_shapes=[pltpu.SemaphoreType.DMA((4,))],
+        scratch_shapes=[
+            pltpu.VMEM((q_here, qlen, hidden), BF16),
+            pltpu.VMEM((hb, dim), F32),
+            pltpu.VMEM((pages_here, slice_len, dim), BF16),
+            pltpu.VMEM((1, q_here), F32),
+            pltpu.SemaphoreType.DMA((4,)),
+            pltpu.SemaphoreType.DMA((4,)),
+        ],
     )(hgrad.reshape(q_here, qlen, hidden), pgrad, pagegrad, losses)
     return losses.reshape(q_here), hgrad, pgrad, pagegrad
 

time: 34 us -> 33.8 us (level)
  no operation moved by 1% of the time
where the time goes in v3:
time: 33.8 us; the launch traced here: 33.6 us
  Pallas kernels  33 us (98%)
  between operations  0.64 us (2%)
    pallas_call x1, Pallas kernels, body(): pl.pallas_call(functools.partial(kernel, groups, members, qlen, nhn, nb),...  30.5 us
    pallas_call x1, Pallas kernels, body(): pl.pallas_call(finish, out_shape=(jax.ShapeDtypeStruct((q_here, qlen, hid...  2.43 us

profile of v3, /device:TPU:1, one launch (start us, length us, event | category | flops | bytes accessed | tf_op | source)
XLA Modules:
  0.0 33.6 jit_solution(2984686061448446708)
XLA Ops:
  0.6 30.5 %shard_map.102 = (f32[1,1]{1,0:T(1,128)}, bf16[32,3584]{1,0:T(8,128)(2,1)}, f32[112,128]{1,0:T(8,128)}, bf16[4,256,128]{2,1,0:T(8,128)(2,1)}) custom-call(bf16[32,3584]{1,0:T(8,128)(2,1)} %bitcast.7, bf16[3584,128]{1,0:T(8,128)(2,1)} %proj_in.1, bf16[4,256,128]{2,1,0:T(8,128)(2,1)} %page_in.1, s32[32]{0:T(128)} %counts_in.1, s32[1,32]{1,0:T(1,128)} %bitcast.9, ...), custom_call_target="tpu_custom_call" | custom-call | tf_op jit(solution)/shard_map/pallas_call | solution.py:421
  31.2 2.4 %shard_map.103 = (bf16[1,32,3584]{2,1,0:T(8,128)(2,1)}, f32[112,128]{1,0:T(8,128)}, bf16[4,256,128]{2,1,0:T(8,128)(2,1)}, f32[1,1]{1,0:T(1,128)}) custom-call(bf16[1,32,3584]{2,1,0:T(8,128)(2,1)} %bitcast.8, f32[112,128]{1,0:T(8,128)} %get-tuple-element.13.b_in, bf16[4,256,128]{2,1,0:T(8,128)(2,1)} %get-tuple-element.14.c_in, f32[1,1]{1,0:T(1,128)} %get-tuple-element.15.d_in), custom_call_target="tpu_custom_call" | custom-call | tf_op jit(solution)/shard_map/pallas_call | solution.py:486
